TPU v7x, 32 devices: a whole 2x2x4 slice. The times are simulated.
32 devices in a mesh: gx: 2 (over y), gy: 4 (over x, core), gz: 4 (over z).
Axes of the slice: x: 2, y: 2, z: 4, core: 2. Of those that a mesh axis runs over, the one named last changes fastest.
Arguments:
- velocity: float32 [3, 64, 128, 512], P(None, 'gx', 'gy', 'gz'), may hold values from -3 to 3
- box_level: float32 [512, 16, 256], P(('gx', 'gy', 'gz')), may hold values from -9 to 9
- corners: int32 [512, 3], P(('gx', 'gy', 'gz')), may hold values from 0 to 112, as said below
- owner_list: int32 [512], P(('gx', 'gy', 'gz')), may hold values from -1 to 15, as said below
Outputs:
- new_velocity: float32 [3, 64, 128, 512], P(None, 'gx', 'gy', 'gz')
- level_sets: float32 [512, 16, 256], P(('gx', 'gy', 'gz'))
- curvature: float32 [512, 16, 256], P(('gx', 'gy', 'gz'))
Inputs may be any that keep to these rules, and one draw needn't show every extreme that they name: `owner_list`: -1 marks an empty slot. The live slots of one device name different helpers, numbered in the order of the devices of its gy+gz group (gy slowest) at the device's own index along gx; every helper is named by exactly 8 slots of its group; a device has 0 to 16 live slots, and some device of every group has 16. `corners`: columns 0, 1, 2 lie in 0 to 16, 16, 112: every box lies inside its home device's block. Boxes may intersect.
All inputs are finite; a program needn't handle non-finite values.
Results may differ from a plain program's by a relative error of at most 0.0003.
Values sent between devices are 32-bit elements; how exact they have to be, the bound alone decides.
A program may use at most 128 MiB of HBM per device.

v0:
```python
import functools
import math

import jax
import jax.numpy as jnp
from jax import lax
from jax.experimental import pallas as pl
from jax.experimental.pallas import tpu as pltpu
from jax.sharding import PartitionSpec as P

ITERS = 12

box_step = 0.25
pseudo_step = 0.3
weno_floor = 1e-06
band_width = 1.5
tension = 2.0
grid_step = 0.2
viscosity = 0.1
normal_floor = 0.5
tiny = 1.1754944e-38

FETCH, GATHER, ADVECT, SECTION, BEND, PUSH, DEPOSIT = 4, 2, 4, 5, 4, 4, 4

MESH = pl.DeviceIdType.MESH


def iota(shape, dim):
    return lax.broadcasted_iota(jnp.int32, shape, dim)


def blend(a, b, c, e, f):
    d1, d2, d3, d4 = a - b, b - c, c - e, e - f
    twice, thrice = 3.0 * d2, 3.0 * d3
    x1, x2, x3 = d1 - d2, d2 - d3, d3 - d4
    y1, y2, y3 = d1 - twice, d2 + d3, thrice - d4
    a1, a2, a3 = [
        (4.0 * weno_floor + (y * y + 13.0 / 3.0 * (x * x))) ** 2
        for x, y in ((x1, y1), (x2, y2), (x3, y3))
    ]
    n1, n2, n3 = a2 * a3, a1 * (6.0 * a3), a1 * (3.0 * a2)
    q1 = 2.0 * d1 - 5.0 * d2
    q2 = d2 + 2.0 * d3
    q3 = d4 - 4.0 * d3
    return c + (n1 * q1 - n2 * q2 + n3 * q3) / (6.0 * (n1 + n2 + n3))


class Box:
    def __init__(self, edge, rows, lanes):
        self.edge, self.rows, self.lanes = edge, rows, lanes
        self.row, self.lane = iota((rows, lanes), 0), iota((rows, lanes), 1)
        j_at, k_at = self.row % edge, self.lane % edge
        self.j_first, self.j_last = j_at == 0, j_at == edge - 1
        self.k_first, self.k_last = k_at == 0, k_at == edge - 1
        self.groups = rows // edge
        self.per = lanes // edge
        self.halves = edge // 8

    def prev_j(self, x):
        return jnp.where(self.j_first, x, pltpu.roll(x, 1, 0))

    def next_j(self, x):
        return jnp.where(self.j_last, x, pltpu.roll(x, self.rows - 1, 0))

    def prev_k(self, x):
        return jnp.where(self.k_first, x, pltpu.roll(x, 1, 1))

    def next_k(self, x):
        return jnp.where(self.k_last, x, pltpu.roll(x, self.lanes - 1, 1))

    def swap_blocks(self, x):
        block = self.lane // self.edge
        for b in (1, 2, 4):
            low = jnp.logical_and((self.row & b) != 0, (block & b) == 0)
            high = jnp.logical_and((self.row & b) == 0, (block & b) != 0)
            down = pltpu.roll(pltpu.roll(x, b, 0), self.lanes - self.edge * b, 1)
            up = pltpu.roll(pltpu.roll(x, self.rows - b, 0), self.edge * b, 1)
            x = jnp.where(low, down, jnp.where(high, up, x))
        return x


def fetch_levels(box, native, lev):
    edge, per = box.edge, box.per

    def fetch(i, carry):
        pieces = [
            native[h, pl.ds(g * per * edge + i, per, stride=edge), :]
            for g in range(box.groups)
            for h in range(box.halves)
        ]
        lev[i] = box.swap_blocks(jnp.concatenate(pieces, axis=0))
        return carry

    lax.fori_loop(0, edge, fetch, 0, unroll=FETCH)


def gather_motion(box, corners, v_ref, mot):
    edge, per, lanes = box.edge, box.per, box.lanes
    slot_lane = iota((edge, lanes), 1) // edge
    for g in range(box.groups):
        places = [[corners[d, g * per + s] for d in range(3)] for s in range(per)]
        turns = [lax.rem(s * edge + lanes - places[s][2], lanes) for s in range(per)]

        def gather(i, carry, g=g, places=places, turns=turns):
            for c in range(3):
                acc = jnp.zeros((edge, lanes), jnp.float32)
                for s in range(per):
                    block = v_ref[c, places[s][0] + i, pl.ds(places[s][1], edge), :]
                    acc = jnp.where(slot_lane == s, pltpu.roll(block, turns[s], 1), acc)
                mot[c, i, pl.ds(g * edge, edge), :] = acc
            return carry

        lax.fori_loop(0, edge, gather, 0, unroll=GATHER)


def advect_levels(box, lev, slope, mot, psa, gain):
    edge = box.edge

    def rise(i, carry):
        slope[i + 3] = lev[i + 1] - lev[i]
        return carry

    zero = jnp.zeros_like(lev[0])
    for n in range(3):
        slope[n] = zero
    lax.fori_loop(0, edge - 1, rise, 0, unroll=5)
    for n in range(3):
        slope[edge + 2 + n] = slope[edge + 1]

    def advect(i, carry):
        here = lev[i]
        change = jnp.zeros_like(here)
        for d in range(3):
            if d == 0:
                slopes = [slope[i + n] for n in range(6)]
            else:
                back, ahead = (box.prev_j, box.next_j) if d == 1 else (box.prev_k, box.next_k)
                mid = here - back(here)
                b1 = back(mid)
                f1 = ahead(mid)
                f2 = ahead(f1)
                slopes = [back(b1), b1, mid, f1, f2, ahead(f2)]
            speed = mot[d, i]
            pos = speed > 0.0
            picks = [jnp.where(pos, slopes[n], slopes[5 - n]) for n in range(5)]
            change = change + speed * blend(*picks)
        out = here - box_step * change
        psa[i] = out
        gain[i] = pseudo_step * out * lax.rsqrt(out * out + 1.0)
        return carry

    lax.fori_loop(0, edge, advect, 0, unroll=ADVECT)


def reinitialize(box, psa, psb, gain):
    edge = box.edge

    def sweep(src, dst):
        for i in range(edge):
            cur = src[i]
            rate = gain[i]
            sign = jnp.where(rate > 0.0, 1.0, -1.0)
            signed = sign * cur
            total = None
            for lo, hi in (
                (src[max(i - 1, 0)], src[min(i + 1, edge - 1)]),
                (box.prev_j(cur), box.next_j(cur)),
                (box.prev_k(cur), box.next_k(cur)),
            ):
                rise = jnp.maximum(signed - jnp.minimum(sign * lo, sign * hi), 0.0)
                total = rise * rise if total is None else total + rise * rise
            root = total * lax.rsqrt(jnp.maximum(total, tiny))
            dst[i] = cur - rate * (root - 1.0)

    def two_sweeps(n, carry):
        sweep(psa, psb)
        sweep(psb, psa)
        return carry

    lax.fori_loop(0, ITERS // 2, two_sweeps, 0)


def pack_z(src, dst, xs, ys, lanes):
    group = iota((ys, lanes), 1) // 4

    def step(x, accs):
        shift = 4 * x + 1
        return tuple(
            jnp.where(group == x, pltpu.roll(src[c, x], shift, 1), accs[c]) for c in range(3)
        )

    accs = lax.fori_loop(
        0, xs, step, tuple(jnp.zeros((ys, lanes), jnp.float32) for _ in range(3)), unroll=8
    )
    for c in range(3):
        dst[c] = accs[c]


def step_kernel(
    sizes, corners, v_hbm, lev_hbm, o_hbm, psi_hbm,
    vel, out, psi_ref, pred, xrecv, ysend, yrecv, zsend, zrecv, comb, lev, slope, mot, psb, gain, native,
    local_sem, lev_sem, out_sem, psi_sem, send_sem, recv_sem,
):
    _, xs, ys, lanes = v_hbm.shape
    box = Box(*lev.shape)
    levels = [
        pltpu.make_async_copy(lev_hbm.at[:, pl.ds(h * lanes, lanes)], native.at[h], lev_sem.at[h])
        for h in range(box.halves)
    ]
    for part in levels:
        part.start()
    load = pltpu.make_async_copy(v_hbm, vel, local_sem)
    load.start()
    ups, downs = [], []
    for axis in ("gx", "gy", "gz"):
        me, n = lax.axis_index(axis), sizes[axis]
        ups.append({axis: lax.rem(me + 1, n)})
        downs.append({axis: lax.rem(me + n - 1, n)})
    barrier = pltpu.get_barrier_semaphore()
    for target in ups + downs:
        pl.semaphore_signal(barrier, inc=1, device_id=target, device_id_type=MESH)
    for part in levels:
        part.wait()
    fetch_levels(box, native, lev)
    load.wait()

    def pack(r, src):
        for c in range(3):
            ysend[r, 0, c] = src[c, :, ys - 1, :]
            ysend[r, 1, c] = src[c, :, 0, :]
        pack_z(src, zsend.at[r], xs, ys, lanes)

    def exchange(r, src):
        copies = []

        def send(n, src, dst, target):
            copy = pltpu.make_async_remote_copy(
                src_ref=src,
                dst_ref=dst,
                send_sem=send_sem.at[r, n],
                recv_sem=recv_sem.at[r, n],
                device_id=target,
                device_id_type=MESH,
            )
            copy.start()
            copies.append(copy)

        send(0, src.at[:, xs - 1], xrecv.at[r, 0], ups[0])
        send(1, src.at[:, 0], xrecv.at[r, 1], downs[0])
        send(2, ysend.at[r, 0], yrecv.at[r, 0], ups[1])
        send(3, ysend.at[r, 1], yrecv.at[r, 1], downs[1])
        send(4, zsend.at[r], zrecv.at[r, 0], ups[2])
        send(5, zsend.at[r], zrecv.at[r, 1], downs[2])
        return copies

    lane = iota((ys, lanes), 1)
    row = iota((ys, lanes), 0)
    quarter = lane % 4

    half = xs // 2

    def store(n):
        part = pl.ds(n * half, half)
        return pltpu.make_async_copy(out.at[:, part], o_hbm.at[:, part], out_sem.at[n])

    def section(r, src, emit, done):
        for c in range(3):
            comb[c] = jnp.where(
                quarter == 0,
                pltpu.roll(zrecv[r, 1, c], lanes - 1, 1),
                pltpu.roll(zrecv[r, 0, c], 1, 1),
            )

        def plane(x, before, after):
            centre = [src[c, x] for c in range(3)]
            for c in range(3):
                mid = centre[c]
                x_lo, x_hi = before(c), after(c)
                y_lo = jnp.where(row == 0, yrecv[r, 0, c, pl.ds(x, 1), :], pltpu.roll(mid, 1, 0))
                y_hi = jnp.where(
                    row == ys - 1, yrecv[r, 1, c, pl.ds(x, 1), :], pltpu.roll(mid, ys - 1, 0)
                )
                halo = pltpu.roll(comb[c], lanes - 1 - 4 * x, 1)
                z_lo = jnp.where(lane == 0, halo, pltpu.roll(mid, 1, 1))
                z_hi = jnp.where(lane == lanes - 1, halo, pltpu.roll(mid, lanes - 1, 1))
                spread = (x_hi + x_lo) + (y_hi + y_lo) + (z_hi + z_lo) - 6.0 * mid
                advect = (
                    centre[0] * (x_hi - x_lo) + centre[1] * (y_hi - y_lo) + centre[2] * (z_hi - z_lo)
                )
                emit(c, x, mid + grid_step * (viscosity * spread - 0.5 * advect))

        def step(x, carry):
            plane(x, lambda c: src[c, x - 1], lambda c: src[c, x + 1])
            return carry

        plane(0, lambda c: xrecv[r, 0, c], lambda c: src[c, 1])
        lax.fori_loop(1, half, step, 0, unroll=SECTION)
        done(0)
        lax.fori_loop(half, xs - 1, step, 0, unroll=SECTION)
        plane(xs - 1, lambda c: src[c, xs - 2], lambda c: xrecv[r, 1, c])
        done(1)

    def first(c, x, value):
        pred[c, x] = value

    def second(c, x, value):
        out[c, x] = 0.5 * (vel[c, x] + value)

    pack(0, vel)
    pl.semaphore_wait(barrier, 6)
    copies = exchange(0, vel)
    gather_motion(box, corners, vel, mot)
    advect_levels(box, lev, slope, mot, psi_ref, gain)
    for copy in copies:
        copy.wait()
    section(0, vel, first, lambda n: None)
    pack(1, pred)
    copies = exchange(1, pred)
    reinitialize(box, psi_ref, psb, gain)
    keep = pltpu.make_async_copy(psi_ref, psi_hbm, psi_sem)
    keep.start()
    for copy in copies:
        copy.wait()
    section(1, pred, second, lambda n: store(n).start())
    store(0).wait()
    store(1).wait()
    keep.wait()


def step_call(velocity, box_level, corners):
    sizes = {axis: lax.axis_size(axis) for axis in ("gx", "gy", "gz")}
    _, xs, ys, lanes = velocity.shape
    slots, edge, plane = box_level.shape
    rows = slots * edge * plane // (edge * lanes)
    vmem = pltpu.VMEM
    f32 = jnp.float32
    return pl.pallas_call(
        functools.partial(step_kernel, sizes),
        out_shape=(
            jax.ShapeDtypeStruct(velocity.shape, f32),
            jax.ShapeDtypeStruct((edge, rows, lanes), f32),
        ),
        in_specs=[
            pl.BlockSpec(memory_space=pltpu.SMEM),
            pl.BlockSpec(memory_space=pl.ANY),
            pl.BlockSpec(memory_space=pl.ANY),
        ],
        out_specs=(pl.BlockSpec(memory_space=pl.ANY), pl.BlockSpec(memory_space=pl.ANY)),
        scratch_shapes=[
            vmem(velocity.shape, f32),
            vmem(velocity.shape, f32),
            vmem((edge, rows, lanes), f32),
            vmem(velocity.shape, f32),
            vmem((2, 2, 3, ys, lanes), f32),
            vmem((2, 2, 3, xs, lanes), f32),
            vmem((2, 2, 3, xs, lanes), f32),
            vmem((2, 3, ys, lanes), f32),
            vmem((2, 2, 3, ys, lanes), f32),
            vmem((3, ys, lanes), f32),
            vmem((edge, rows, lanes), f32),
            vmem((edge + 5, rows, lanes), f32),
            vmem((3, edge, rows, lanes), f32),
            vmem((edge, rows, lanes), f32),
            vmem((edge, rows, lanes), f32),
            vmem((plane // lanes, slots * edge, lanes), f32),
            pltpu.SemaphoreType.DMA(()),
            pltpu.SemaphoreType.DMA((plane // lanes,)),
            pltpu.SemaphoreType.DMA((2,)),
            pltpu.SemaphoreType.DMA(()),
            pltpu.SemaphoreType.DMA((2, 6)),
            pltpu.SemaphoreType.DMA((2, 6)),
        ],
        compiler_params=pltpu.CompilerParams(collective_id=0, has_side_effects=True),
    )(corners, velocity, box_level.reshape(slots * edge, plane))


def force_kernel(
    corners, owners, psi, step_hbm, o_hbm, set_hbm, ben_hbm,
    o_ref, force, part, nrm, native_a, native_b, sem, out_sem, small_sem,
):
    load = pltpu.make_async_copy(step_hbm, o_ref, sem)
    load.start()
    box = Box(*psi.shape)
    edge, per, groups, lanes = box.edge, box.per, box.groups, box.lanes

    def write(ref, i, value):
        value = box.swap_blocks(value)
        for g in range(groups):
            for h in range(box.halves):
                at = g * edge + h * 8
                ref[h, pl.ds(g * per * edge + i, per, stride=edge), :] = value[at : at + 8]

    alive = jnp.zeros((box.rows, lanes), jnp.float32)
    owner_at = (box.row // edge) * per + box.lane // edge
    for s in range(groups * per):
        alive = jnp.where(owner_at == s, jnp.where(owners[s] >= 0, 1.0, 0.0), alive)

    def bend(i, carry):
        cur = psi[i]
        c0 = 0.5 * (psi[jnp.minimum(i + 1, edge - 1)] - psi[jnp.maximum(i - 1, 0)])
        c1 = 0.5 * (box.next_j(cur) - box.prev_j(cur))
        c2 = 0.5 * (box.next_k(cur) - box.prev_k(cur))
        inverse = lax.rsqrt(jnp.maximum(c0 * c0 + c1 * c1 + c2 * c2, normal_floor * normal_floor))
        n1, n2 = c1 * inverse, c2 * inverse
        nrm[i] = c0 * inverse
        part[i] = 0.5 * (box.next_j(n1) - box.prev_j(n1)) + 0.5 * (box.next_k(n2) - box.prev_k(n2))
        force[0, i] = c0
        force[1, i] = c1
        force[2, i] = c2
        return carry

    lax.fori_loop(0, edge, bend, 0, unroll=BEND)

    def push(i, carry):
        level = psi[i] * alive
        curve = (
            part[i] + 0.5 * (nrm[jnp.minimum(i + 1, edge - 1)] - nrm[jnp.maximum(i - 1, 0)])
        ) * alive
        write(native_a, i, level)
        write(native_b, i, curve)
        ratio = level * (1.0 / band_width)
        scale = grid_step * tension / (band_width * math.sqrt(math.pi))
        strength = scale * curve * jnp.exp(-(ratio * ratio)) * alive
        for d in range(3):
            force[d, i] = force[d, i] * strength
        return carry

    lax.fori_loop(0, edge, push, 0, unroll=PUSH)
    stores = []
    for h in range(box.halves):
        part_h = pl.ds(h * lanes, lanes)
        stores.append(pltpu.make_async_copy(native_a.at[h], set_hbm.at[:, part_h], small_sem.at[0, h]))
        stores.append(pltpu.make_async_copy(native_b.at[h], ben_hbm.at[:, part_h], small_sem.at[1, h]))
    for copy in stores:
        copy.start()

    load.wait()
    wide = iota((edge, lanes), 1)

    def deposit_slot(n, carry):
        g, s = n // per, n % per
        ax, ay, az = corners[0, n], corners[1, n], corners[2, n]
        turn = lax.rem(az + lanes - s * edge, lanes)
        inside = jnp.logical_and(wide >= az, wide < az + edge)
        first_row = pl.multiple_of(g * edge, edge)

        for i in range(0, edge, DEPOSIT):
            spots = [(c, i + t) for t in range(DEPOSIT) for c in range(3)]
            blocks = [pltpu.roll(force[c, q, pl.ds(first_row, edge), :], turn, 1) for c, q in spots]
            olds = [o_ref[c, ax + q, pl.ds(ay, edge), :] for c, q in spots]
            news = [old + jnp.where(inside, block, 0.0) for old, block in zip(olds, blocks)]
            for (c, q), new in zip(spots, news):
                o_ref[c, ax + q, pl.ds(ay, edge), :] = new
        return carry

    lax.fori_loop(0, groups * per, deposit_slot, 0)
    for c in range(3):
        stores.append(pltpu.make_async_copy(o_ref.at[c], o_hbm.at[c], out_sem.at[c]))
        stores[-1].start()
    for copy in stores:
        copy.wait()


def force_call(shapes, psi, corners, owner_list, stepped):
    slots, edge, plane = shapes
    rows, lanes = psi.shape[1:]
    flat = (slots * edge, plane)
    f32 = jnp.float32
    whole = pl.BlockSpec(memory_space=pltpu.VMEM)
    smem = pl.BlockSpec(memory_space=pltpu.SMEM)
    field = pltpu.VMEM((edge, rows, lanes), f32)
    native = pltpu.VMEM((plane // lanes, slots * edge, lanes), f32)
    result, settled, bending = pl.pallas_call(
        force_kernel,
        out_shape=(
            jax.ShapeDtypeStruct(stepped.shape, f32),
            jax.ShapeDtypeStruct(flat, f32),
            jax.ShapeDtypeStruct(flat, f32),
        ),
        in_specs=[smem, smem, whole, pl.BlockSpec(memory_space=pl.ANY)],
        out_specs=(pl.BlockSpec(memory_space=pl.ANY),) * 3,
        scratch_shapes=[
            pltpu.VMEM(stepped.shape, f32),
            pltpu.VMEM((3, edge, rows, lanes), f32),
            field,
            field,
            native,
            native,
            pltpu.SemaphoreType.DMA(()),
            pltpu.SemaphoreType.DMA((3,)),
            pltpu.SemaphoreType.DMA((2, plane // lanes)),
        ],
    )(corners, owner_list, psi, stepped)
    return result, settled.reshape(shapes), bending.reshape(shapes)


def local(velocity, box_level, corners, owner_list):
    turned = corners.T
    stepped, psi = step_call(velocity, box_level, turned)
    return force_call(box_level.shape, psi, turned, owner_list, stepped)


def solution(mesh):
    placed = (
        P(None, "gx", "gy", "gz"),
        P(("gx", "gy", "gz"), None, None),
        P(("gx", "gy", "gz"), None),
        P(("gx", "gy", "gz")),
    )
    return jax.shard_map(
        local,
        mesh=mesh,
        in_specs=placed,
        out_specs=(
            P(None, "gx", "gy", "gz"),
            P(("gx", "gy", "gz"), None, None),
            P(("gx", "gy", "gz"), None, None),
        ),
        check_vma=False,
    )
```

profile of v0, /device:TPU:0, one launch (start us, length us, event | category | flops | bytes accessed | tf_op | source)
XLA Modules:
  0.0 30.0 jit_solution(17200234636471305571)
XLA Ops:
  0.6 22.1 %shard_map.67 = (f32[3,32,32,128]{3,2,1,0:T(8,128)}, f32[16,32,128]{2,1,0:T(8,128)}) custom-call(s32[3,16]{1,0:T(4,128)} %bitcast.5, f32[3,32,32,128]{3,2,1,0:T(8,128)} %v_hbm.1, f32[256,256]{1,0:T(8,128)} %bitcast.4), custom_call_target="tpu_custom_call" | custom-call | tf_op jit(solution)/shard_map/pallas_call | solution.py:337
  22.7 7.3 %shard_map.68 = (f32[3,32,32,128]{3,2,1,0:T(8,128)}, f32[256,256]{1,0:T(8,128)}, f32[256,256]{1,0:T(8,128)}) custom-call(s32[3,16]{1,0:T(4,128)} %bitcast.6, s32[16]{0:T(128)} %owners.1, f32[16,32,128]{2,1,0:T(8,128)} %get-tuple-element.8.psi, f32[3,32,32,128]{3,2,1,0:T(8,128)} %get-tuple-element.9.step_hbm), custom_call_target="tpu_custom_call" | custom-call | tf_op jit(solution)/shard_map/pallas_call | solution.py:473
where the time goes:
time: 30.2 us; the launch traced here: 30 us
  Pallas kernels  29.4 us (97%)
  between operations  0.64 us (2%)
    pallas_call x1, Pallas kernels, step_call(): pl.pallas_call(functools.partial(step_kernel, sizes), out_shape=(jax.Shap...  22.1 us
    pallas_call x1, Pallas kernels, force_call(): pl.pallas_call(force_kernel, out_shape=(jax.ShapeDtypeStruct(stepped.shap...  7.33 us

commit v1 on v0

v1 whole, which is shorter than its diff:
```python
import functools
import math

import jax
import jax.numpy as jnp
from jax import lax
from jax.experimental import pallas as pl
from jax.experimental.pallas import tpu as pltpu
from jax.sharding import PartitionSpec as P

ITERS = 12

box_step = 0.25
pseudo_step = 0.3
weno_floor = 1e-06
band_width = 1.5
tension = 2.0
grid_step = 0.2
viscosity = 0.1
normal_floor = 0.5
speck = 1.1e-19

SUB = 8
CHUNK = 8
DEPOSIT = 4
MIB = 1 << 20

MESH = pl.DeviceIdType.MESH
f32, bf16 = jnp.float32, jnp.bfloat16


def iota(shape, dim):
    return lax.broadcasted_iota(jnp.int32, shape, dim)


def halves(x):
    high = x.astype(bf16)
    return jnp.concatenate([high, (x - high.astype(f32)).astype(bf16)], axis=1)


def ones(mask):
    return jnp.where(mask, 1.0, 0.0).astype(bf16)


class Box:
    def __init__(self, edge, lanes, slots):
        self.edge, self.lanes = edge, lanes
        self.per = lanes // edge
        self.groups = slots // self.per
        self.halves = edge // SUB
        self.here = pl.ds(SUB, edge)
        self.below = pl.ds(SUB - 1, edge)
        self.above = pl.ds(SUB + 1, edge)
        self.block8 = iota((SUB, lanes), 1) // edge
        self.row8 = iota((SUB, lanes), 0)
        self.block = iota((edge, lanes), 1) // edge
        k_at = iota((edge, lanes), 1) % edge
        self.k_first, self.k_last = k_at == 0, k_at == edge - 1
        self.k_at = k_at

    def prev(self, x, n=1):
        return pltpu.roll(x, n, 1)

    def next(self, x, n=1):
        return pltpu.roll(x, self.lanes - n, 1)

    def swap_blocks(self, x):
        x = pltpu.roll(x, 0, 1, stride=self.edge, stride_axis=0)
        for b in (1, 2, 4):
            x = jnp.where((self.block8 & b) != 0, pltpu.roll(x, SUB - b, 0), x)
        x = pltpu.roll(x, 0, 1, stride=self.edge, stride_axis=0)
        x = pltpu.roll(x, 4, 0)
        for b in (1, 2):
            x = jnp.where((self.row8 & b) != 0, pltpu.roll(x, b, 0), pltpu.roll(x, SUB - b, 0))
        return pltpu.roll(x, 1, 0)

    def put(self, ref, i, g, value):
        last = SUB + self.edge
        ref[i, g, self.here] = value
        ref[i, g, SUB - 1 : SUB] = value[:1]
        ref[i, g, last : last + 1] = value[self.edge - 1 :]


def fetch_levels(box, native, lev):
    edge, per = box.edge, box.per

    def fetch(i, carry):
        for g in range(box.groups):
            pieces = [
                box.swap_blocks(native[h, pl.ds(g * per * edge + i, per, stride=edge), :])
                for h in range(box.halves)
            ]
            box.put(lev, i, g, 2.0 * jnp.concatenate(pieces, axis=0))
        return carry

    lax.fori_loop(0, edge, fetch, 0, unroll=4)


def window_matrix(box, corners):
    lanes, edge = box.lanes, box.edge
    columns = []
    for g in range(box.groups):
        block = iota((1, lanes), 1) // edge
        first = jnp.zeros((1, lanes), jnp.int32)
        for s in range(box.per):
            first = jnp.where(block == s, corners[2, g * box.per + s], first)
        wanted = first + iota((1, lanes), 1) % edge
        columns.append(ones(iota((lanes, lanes), 0) == wanted))
    both = jnp.concatenate(columns, axis=1)
    return jnp.concatenate([both, both], axis=0)


def shift_matrix(lanes):
    z, l = iota((lanes, lanes), 0), iota((lanes, lanes), 1)
    both = jnp.concatenate([ones(z == l - 1), ones(z == l + 1)], axis=1)
    return jnp.concatenate([both, both], axis=0)


def gather_motion(box, corners, wide, mot):
    edge, per = box.edge, box.per
    for g in range(box.groups):
        places = [[corners[d, g * per + s] for d in range(2)] for s in range(per)]

        def gather(i, carry, g=g, places=places):
            for c in range(3):
                acc = None
                for s in range(per):
                    rows = wide[c, g, places[s][0] + i, pl.ds(places[s][1], edge), :]
                    acc = rows if acc is None else jnp.where(box.block == s, rows, acc)
                mot[c, i, g] = acc
            return carry

        lax.fori_loop(0, edge, gather, 0, unroll=2)


def lean(e1, e2, e3, e4):
    floor = 3.0 * weno_floor
    s2, s3 = e2 * e2, e3 * e3
    b1 = e1 * (e1 - 2.75 * e2) + (2.5 * s2 + floor)
    b2 = e2 * (e2 - 1.25 * e3) + (s3 + floor)
    b3 = e4 * (e4 - 2.75 * e3) + (2.5 * s3 + floor)
    a1, a2, a3 = 3.0 * (b1 * b1), b2 * b2, b3 * b3
    t = 2.0 * e3
    p = a2 * a3
    top = p * (e1 - 2.5 * e2) + a1 * (a2 * (0.5 * e4 - t) - a3 * (e2 + t))
    return top, p + a1 * (a2 + 2.0 * a3)


def advect_levels(box, lev, mi, di, mj, dj, mot, psa, sign, rate):
    edge, here, below, above = box.edge, box.here, box.below, box.above
    zero = jnp.zeros((edge, box.lanes), f32)
    last = SUB + edge

    for g in range(box.groups):
        mi[0, g] = zero
        for n in (0, 1, edge + 1, edge + 2, edge + 3):
            di[n, g] = zero

    def rise(i, carry):
        for g in range(box.groups):
            @pl.when(i > 0)
            def _(g=g):
                mi[i, g] = lev[i, g, here] - lev[i - 1, g, here]

            step = lev[i, g, here] - lev[i, g, below]
            mj[i, g, here] = step
            mj[i, g, last : last + 1] = step[edge - 1 :]
        return carry

    lax.fori_loop(0, edge, rise, 0, unroll=True)
    for g in range(box.groups):
        mi[edge, g] = mi[edge - 1, g]

    def bow(i, carry):
        for g in range(box.groups):
            if_last = mi[i, g] - mi[i + 1, g]
            di[i + 2, g] = if_last
            dj[i, g, pl.ds(0, SUB)] = zero[:SUB]
            dj[i, g, pl.ds(last, SUB)] = zero[:SUB]
            dj[i, g, here] = mj[i, g, here] - mj[i, g, above]
        return carry

    lax.fori_loop(0, edge, bow, 0, unroll=4)

    k_low2 = box.k_at >= 2
    k_up1 = box.k_at < edge - 1
    k_up2 = box.k_at < edge - 2

    def advect(i, carry):
        for g in range(box.groups):
            level = lev[i, g, here]
            drift = turn = None
            for d in range(3):
                if d == 0:
                    m0, m1 = mi[i, g], mi[i + 1, g]
                    ds = [di[i + n, g] for n in range(5)]
                elif d == 1:
                    m0, m1 = mj[i, g, here], mj[i, g, above]
                    ds = [dj[i, g, pl.ds(SUB - 2 + n, edge)] for n in range(5)]
                else:
                    m0 = jnp.where(box.k_first, 0.0, level - box.prev(level))
                    m1 = jnp.where(box.k_last, m0, box.next(m0))
                    mid = m0 - m1
                    ds = [
                        jnp.where(k_low2, box.prev(mid, 2), 0.0),
                        box.prev(mid, 1),
                        mid,
                        jnp.where(k_up1, box.next(mid, 1), 0.0),
                        jnp.where(k_up2, box.next(mid, 2), 0.0),
                    ]
                speed = mot[d, i, g]
                pos = speed > 0.0
                e1 = jnp.where(pos, ds[0], ds[4])
                e2 = jnp.where(pos, ds[1], ds[3])
                e4 = jnp.where(pos, ds[3], ds[1])
                top, bottom = lean(e1, e2, ds[2], e4)
                part = speed * jnp.where(pos, m0, m1)
                extra = jnp.abs(speed) * (top / bottom)
                drift = part if drift is None else drift + part
                turn = extra if turn is None else turn + extra
            out = 0.5 * level - (0.5 * box_step) * drift - (box_step / 6.0) * turn
            box.put(psa, i, g, out)
            sign[i, g] = jnp.where(out > 0.0, 1.0, -1.0)
            rate[i, g] = pseudo_step * out * lax.rsqrt(out * out + 1.0)
        return carry

    lax.fori_loop(0, edge, advect, 0, unroll=2)


def reinitialize(box, psa, psb, sign, rate):
    edge, here, below, above = box.edge, box.here, box.below, box.above
    low = jnp.where(box.k_first, 0.0, 1.0)
    high = jnp.where(box.k_last, 0.0, 1.0)

    def sweep(src, dst):
        for i in range(edge):
            for g in range(box.groups):
                cur = src[i, g, here]
                s, r = sign[i, g], rate[i, g]
                signed = s * cur
                x = signed - jnp.minimum(
                    s * src[max(i - 1, 0), g, here], s * src[min(i + 1, edge - 1), g, here]
                )
                y = signed - jnp.minimum(s * src[i, g, below], s * src[i, g, above])
                z = jnp.maximum(
                    (s * low) * (cur - box.prev(cur)), (s * high) * (cur - box.next(cur))
                )
                x = jnp.maximum(x, speck)
                y, z = jnp.maximum(y, 0.0), jnp.maximum(z, 0.0)
                total = x * x + y * y + z * z
                box.put(dst, i, g, (cur + r) - r * (total * lax.rsqrt(total)))

    def two_sweeps(n, carry):
        sweep(psa, psb)
        sweep(psb, psa)
        return carry

    lax.fori_loop(0, ITERS // 2, two_sweeps, 0)


def curve_levels(box, owners, psi, nx, ny, part, force, native_a, native_b):
    edge, per, here, below, above = box.edge, box.per, box.here, box.below, box.above

    def spread(x):
        return jnp.where(box.k_last, x, box.next(x)) - jnp.where(box.k_first, x, box.prev(x))

    def bend(i, carry):
        for g in range(box.groups):
            cur = psi[i, g, here]
            c0 = psi[jnp.minimum(i + 1, edge - 1), g, here] - psi[jnp.maximum(i - 1, 0), g, here]
            c1 = psi[i, g, above] - psi[i, g, below]
            c2 = spread(cur)
            floor = 4.0 * normal_floor * normal_floor
            inverse = lax.rsqrt(jnp.maximum(c0 * c0 + c1 * c1 + c2 * c2, floor))
            nx[i, g] = c0 * inverse
            box.put(ny, i, g, c1 * inverse)
            part[i, g] = spread(c2 * inverse)
            for d, c in enumerate((c0, c1, c2)):
                force[d, i, g] = c
        return carry

    lax.fori_loop(0, edge, bend, 0, unroll=2)

    alive = []
    for g in range(box.groups):
        live = jnp.zeros((edge, box.lanes), f32)
        for s in range(per):
            on = jnp.where(owners[g * per + s] >= 0, 1.0, 0.0)
            live = jnp.where(box.block == s, on, live)
        alive.append(live)

    def push(i, carry):
        for g in range(box.groups):
            live = alive[g]
            level = psi[i, g, here] * live
            ends = nx[jnp.minimum(i + 1, edge - 1), g] - nx[jnp.maximum(i - 1, 0), g]
            curve = (0.5 * live) * (ends + (ny[i, g, above] - ny[i, g, below]) + part[i, g])
            for h in range(box.halves):
                at = pl.ds(g * per * edge + i, per, stride=edge)
                rows = slice(h * SUB, (h + 1) * SUB)
                native_a[h, at, :] = box.swap_blocks(level[rows])
                native_b[h, at, :] = box.swap_blocks(curve[rows])
            ratio = level * (1.0 / band_width)
            scale = 0.5 * grid_step * tension / (band_width * math.sqrt(math.pi))
            strength = scale * curve * jnp.exp(-(ratio * ratio)) * live
            for d in range(3):
                force[d, i, g] = force[d, i, g] * strength
        return carry

    lax.fori_loop(0, edge, push, 0, unroll=2)


class Grid:
    def __init__(self, xs, ys, lanes):
        self.xs, self.ys, self.lanes = xs, ys, lanes
        self.here = pl.ds(SUB, ys)
        self.below = pl.ds(SUB - 1, ys)
        self.above = pl.ds(SUB + 1, ys)
        self.rows = ys + 2 * SUB
        self.shape = (3, xs + 2, self.rows, lanes)
        self.lane = iota((ys, lanes), 1)
        self.group = self.lane // 4

    def row_of(self, ref, c, x, row):
        flat = ref.reshape(3 * (self.xs + 2) * self.rows, self.lanes)
        return flat.at[pl.ds((c * (self.xs + 2) + x) * self.rows + row, SUB, stride=self.rows), :]

    def fill_rows(self, ref, low, high):
        for c in range(3):
            for x in range(0, self.xs, SUB):
                part = pl.ds(x, SUB)
                self.row_of(ref, c, x + 1, SUB - 1)[...] = low[c, part]
                self.row_of(ref, c, x + 1, SUB + self.ys)[...] = high[c, part]

    def take_rows(self, ref, ysend):
        for c in range(3):
            for x in range(0, self.xs, SUB):
                part = pl.ds(x, SUB)
                ysend[0, c, part] = self.row_of(ref, c, x + 1, SUB + self.ys - 1)[...]
                ysend[1, c, part] = self.row_of(ref, c, x + 1, SUB)[...]

    def combine(self, zlow, zhigh, comb):
        for c in range(3):
            comb[c] = jnp.where(
                self.lane % 4 == 0,
                pltpu.roll(zhigh[c], self.lanes - 1, 1),
                pltpu.roll(zlow[c], 1, 1),
            )

    def packed(self, value, x, acc):
        return jnp.where(self.group == x, pltpu.roll(value, 4 * x + 1, 1), acc)

    def shift(self, src, shifts, near, slot, first):
        left = jnp.concatenate(
            [halves(src[c, 1 + first + n, self.here]) for c in range(3) for n in range(CHUNK)], axis=0
        )
        both = jnp.dot(left, shifts[...], preferred_element_type=f32)
        for c in range(3):
            for n in range(CHUNK):
                at = (c * CHUNK + n) * self.ys
                for e in range(2):
                    near[slot, c, n, e] = both[at : at + self.ys, e * self.lanes : (e + 1) * self.lanes]

    def section(self, src, comb, shifts, near, scale, emit):
        h = scale * grid_step * viscosity
        chunks = self.xs // CHUNK

        def chunk(t, carry):
            slot = t % 2
            self.shift(src, shifts, near, 1 - slot, CHUNK * jnp.minimum(t + 1, chunks - 1))
            for n in range(CHUNK):
                x = CHUNK * t + n
                centre = [src[c, x + 1, self.here] for c in range(3)]
                w = [(0.5 * scale * grid_step) * v for v in centre]
                up, down = [h - v for v in w], [h + v for v in w]
                rim = jnp.where(self.lane == 0, down[2], jnp.where(self.lane == self.lanes - 1, up[2], 0.0))
                for c in range(3):
                    halo = pltpu.roll(comb[c], self.lanes - 1 - 4 * x, 1)
                    value = (
                        (scale - 6.0 * h) * centre[c]
                        + up[0] * src[c, x + 2, self.here]
                        + down[0] * src[c, x, self.here]
                        + up[1] * src[c, x + 1, self.above]
                        + down[1] * src[c, x + 1, self.below]
                        + up[2] * near[slot, c, n, 1]
                        + down[2] * near[slot, c, n, 0]
                        + rim * halo
                    )
                    emit(c, x, value)
            return carry

        lax.fori_loop(0, chunks, chunk, 0)


def step_kernel(
    sizes, corners, owners, v_hbm, lev_hbm,
    vel, pred, yrecv1, zrecv1, force, native_a, native_b,
    yrecv0, zrecv0, ysend, zsend, comb, near, shifts, windows, wide,
    native, lev, mi, di, mj, dj, mot, psa, psb, sign, rate,
    local_sem, lev_sem, send_sem, recv_sem,
):
    _, xs, ys, lanes = v_hbm.shape
    grid = Grid(xs, ys, lanes)
    slots = corners.shape[1]
    edge = lev.shape[0]
    box = Box(edge, lanes, slots)
    inner = pl.ds(1, xs)
    levels = [
        pltpu.make_async_copy(lev_hbm.at[:, pl.ds(h * lanes, lanes)], native.at[h], lev_sem.at[h])
        for h in range(box.halves)
    ]
    for part in levels:
        part.start()
    load = pltpu.make_async_copy(v_hbm, vel.at[:, inner, grid.here], local_sem)
    load.start()
    ups, downs = [], []
    for axis in ("gx", "gy", "gz"):
        me, n = lax.axis_index(axis), sizes[axis]
        ups.append({axis: lax.rem(me + 1, n)})
        downs.append({axis: lax.rem(me + n - 1, n)})
    barrier = pltpu.get_barrier_semaphore()
    for target in ups + downs:
        pl.semaphore_signal(barrier, inc=1, device_id=target, device_id_type=MESH)
    shifts[...] = shift_matrix(lanes)
    windows[...] = window_matrix(box, corners)
    for part in levels:
        part.wait()
    fetch_levels(box, native, lev)
    load.wait()

    def exchange(r, src, yrecv, zrecv):
        copies = []

        def send(n, src, dst, target):
            copy = pltpu.make_async_remote_copy(
                src_ref=src,
                dst_ref=dst,
                send_sem=send_sem.at[r, n],
                recv_sem=recv_sem.at[r, n],
                device_id=target,
                device_id_type=MESH,
            )
            copy.start()
            copies.append(copy)

        send(0, src.at[:, xs, grid.here], src.at[:, 0, grid.here], ups[0])
        send(1, src.at[:, 1, grid.here], src.at[:, xs + 1, grid.here], downs[0])
        send(2, ysend.at[r, 0], yrecv.at[0], ups[1])
        send(3, ysend.at[r, 1], yrecv.at[1], downs[1])
        send(4, zsend.at[r], zrecv.at[0], ups[2])
        send(5, zsend.at[r], zrecv.at[1], downs[2])
        return copies

    for c in range(3):
        zsend[0, c] = jnp.zeros((ys, lanes), f32)
        zsend[1, c] = jnp.zeros((ys, lanes), f32)
    span = xs // 2

    def spread(t, carry):
        left = []
        for c in range(3):
            acc = zsend[0, c]
            for n in range(span):
                x = span * t + n
                value = vel[c, x + 1, grid.here]
                left.append(halves(value))
                acc = grid.packed(value, x, acc)
            zsend[0, c] = acc
        both = jnp.dot(jnp.concatenate(left, axis=0), windows[...], preferred_element_type=f32)
        for c in range(3):
            for n in range(span):
                at = (c * span + n) * ys
                for g in range(box.groups):
                    wide[c, g, span * t + n] = both[at : at + ys, g * lanes : (g + 1) * lanes]
        return carry

    lax.fori_loop(0, xs // span, spread, 0)
    grid.take_rows(vel, ysend.at[0])
    pl.semaphore_wait(barrier, 6)
    copies = exchange(0, vel, yrecv0, zrecv0)
    gather_motion(box, corners, wide, mot)
    advect_levels(box, lev, mi, di, mj, dj, mot, psa, sign, rate)
    grid.shift(vel, shifts, near, 0, 0)
    for copy in copies:
        copy.wait()
    grid.fill_rows(vel, yrecv0.at[0], yrecv0.at[1])
    grid.combine(zrecv0.at[0], zrecv0.at[1], comb)

    def first(c, x, value):
        pred[c, x + 1, grid.here] = value
        zsend[1, c] = grid.packed(value, x, zsend[1, c])

    grid.section(vel, comb, shifts, near, 1.0, first)
    grid.take_rows(pred, ysend.at[1])
    copies = exchange(1, pred, yrecv1, zrecv1)
    reinitialize(box, psa, psb, sign, rate)
    curve_levels(box, owners, psa, mi, mj, di, force, native_a, native_b)
    for copy in copies:
        copy.wait()


def kept(x):
    return pltpu.with_memory_space_constraint(x, pltpu.HBM)


def step_call(velocity, box_level, corners, owner_list):
    sizes = {axis: lax.axis_size(axis) for axis in ("gx", "gy", "gz")}
    _, xs, ys, lanes = velocity.shape
    slots, edge, plane = box_level.shape
    groups = slots * edge // lanes
    vmem = pltpu.VMEM
    grid_shape = (3, xs + 2, ys + 2 * SUB, lanes)
    tall = (edge, groups, edge + 2 * SUB, lanes)
    flat = (edge, groups, edge, lanes)
    native = (plane // lanes, slots * edge, lanes)
    smem = pl.BlockSpec(memory_space=pltpu.SMEM)
    return pl.pallas_call(
        functools.partial(step_kernel, sizes),
        out_shape=(
            vmem(grid_shape, f32),
            vmem(grid_shape, f32),
            vmem((2, 3, xs, lanes), f32),
            vmem((2, 3, ys, lanes), f32),
            vmem((3,) + flat, f32),
            vmem(native, f32),
            vmem(native, f32),
        ),
        in_specs=[smem, smem, pl.BlockSpec(memory_space=pltpu.HBM), pl.BlockSpec(memory_space=pltpu.HBM)],
        out_specs=(pl.BlockSpec(memory_space=vmem),) * 7,
        scratch_shapes=[
            vmem((2, 3, xs, lanes), f32),
            vmem((2, 3, ys, lanes), f32),
            vmem((2, 2, 3, xs, lanes), f32),
            vmem((2, 3, ys, lanes), f32),
            vmem((3, ys, lanes), f32),
            vmem((2, 3, CHUNK, 2, ys, lanes), f32),
            vmem((2 * lanes, 2 * lanes), bf16),
            vmem((2 * lanes, groups * lanes), bf16),
            vmem((3, groups, xs, ys, lanes), f32),
            vmem(native, f32),
            vmem(tall, f32),
            vmem((edge + 1,) + flat[1:], f32),
            vmem((edge + 4,) + flat[1:], f32),
            vmem(tall, f32),
            vmem(tall, f32),
            vmem((3,) + flat, f32),
            vmem(tall, f32),
            vmem(tall, f32),
            vmem(flat, f32),
            vmem(flat, f32),
            pltpu.SemaphoreType.DMA(()),
            pltpu.SemaphoreType.DMA((plane // lanes,)),
            pltpu.SemaphoreType.DMA((2, 6)),
            pltpu.SemaphoreType.DMA((2, 6)),
        ],
        compiler_params=pltpu.CompilerParams(
            collective_id=0, has_side_effects=True, vmem_limit_bytes=36 * MIB
        ),
    )(corners, owner_list, kept(velocity), kept(box_level.reshape(slots * edge, plane)))


def force_kernel(
    corners, vel, pred, yrecv, zrecv, force, native_a, native_b,
    o_hbm, set_hbm, ben_hbm,
    src, o_ref, comb, near, shifts, out_sem, small_sem,
):
    _, xs, ys, lanes = o_ref.shape
    grid = Grid(xs, ys, lanes)
    slots = corners.shape[1]
    edge = force.shape[1]
    box = Box(edge, lanes, slots)
    per = box.per
    stores = []
    for h in range(box.halves):
        part_h = pl.ds(h * lanes, lanes)
        stores.append(pltpu.make_async_copy(native_a.at[h], set_hbm.at[:, part_h], small_sem.at[0, h]))
        stores.append(pltpu.make_async_copy(native_b.at[h], ben_hbm.at[:, part_h], small_sem.at[1, h]))
    for copy in stores:
        copy.start()
    shifts[...] = shift_matrix(lanes)
    grid.combine(zrecv.at[0], zrecv.at[1], comb)
    grid.shift(pred, shifts, near, 0, 0)

    def second(c, x, value):
        o_ref[c, x] = 0.5 * vel[c, x + 1, grid.here] + value

    grid.fill_rows(pred, yrecv.at[0], yrecv.at[1])
    grid.section(pred, comb, shifts, near, 0.5, second)

    wide = iota((edge, lanes), 1)

    def deposit_slot(n, carry):
        g, s = n // per, n % per
        ax, ay, az = corners[0, n], corners[1, n], corners[2, n]
        turn = lax.rem(az + lanes - s * edge, lanes)
        inside = jnp.logical_and(wide >= az, wide < az + edge)

        for i in range(0, edge, DEPOSIT):
            spots = [(c, i + t) for t in range(DEPOSIT) for c in range(3)]
            blocks = [pltpu.roll(force[c, q, g], turn, 1) for c, q in spots]
            olds = [o_ref[c, ax + q, pl.ds(ay, edge), :] for c, q in spots]
            news = [old + jnp.where(inside, block, 0.0) for old, block in zip(olds, blocks)]
            for (c, q), new in zip(spots, news):
                o_ref[c, ax + q, pl.ds(ay, edge), :] = new
        return carry

    lax.fori_loop(0, slots, deposit_slot, 0)
    for c in range(3):
        stores.append(pltpu.make_async_copy(o_ref.at[c], o_hbm.at[c], out_sem.at[c]))
        stores[-1].start()
    for copy in stores:
        copy.wait()


def force_call(shapes, block, corners, handed):
    slots, edge, plane = shapes
    _, xs, ys, lanes = block
    flat = (slots * edge, plane)
    whole = pl.BlockSpec(memory_space=pltpu.VMEM)
    smem = pl.BlockSpec(memory_space=pltpu.SMEM)
    handed = [pltpu.with_memory_space_constraint(a, pltpu.VMEM) for a in handed]
    result, settled, bending = pl.pallas_call(
        force_kernel,
        out_shape=(
            jax.ShapeDtypeStruct(block, f32),
            jax.ShapeDtypeStruct(flat, f32),
            jax.ShapeDtypeStruct(flat, f32),
        ),
        in_specs=[smem] + [whole] * 7,
        out_specs=(pl.BlockSpec(memory_space=pltpu.HBM),) * 3,
        scratch_shapes=[
            pltpu.VMEM((SUB, lanes), f32),
            pltpu.VMEM(block, f32),
            pltpu.VMEM((3, ys, lanes), f32),
            pltpu.VMEM((2, 3, CHUNK, 2, ys, lanes), f32),
            pltpu.VMEM((2 * lanes, 2 * lanes), bf16),
            pltpu.SemaphoreType.DMA((3,)),
            pltpu.SemaphoreType.DMA((2, plane // lanes)),
        ],
        compiler_params=pltpu.CompilerParams(vmem_limit_bytes=24 * MIB),
    )(corners, *handed)
    return result, settled.reshape(shapes), bending.reshape(shapes)


def local(velocity, box_level, corners, owner_list):
    turned, owner_list = kept(corners.T), kept(owner_list)
    handed = step_call(velocity, box_level, turned, owner_list)
    return force_call(box_level.shape, velocity.shape, turned, handed)


def solution(mesh):
    placed = (
        P(None, "gx", "gy", "gz"),
        P(("gx", "gy", "gz"), None, None),
        P(("gx", "gy", "gz"), None),
        P(("gx", "gy", "gz")),
    )
    return jax.shard_map(
        local,
        mesh=mesh,
        in_specs=placed,
        out_specs=(
            P(None, "gx", "gy", "gz"),
            P(("gx", "gy", "gz"), None, None),
            P(("gx", "gy", "gz"), None, None),
        ),
        check_vma=False,
    )
```

time: 30.2 us -> 27.2 us (0.901)
  Pallas kernels: 29.4 us -> 26.4 us
    pallas_call x2, Pallas kernels: 29.4 us -> 26.4 us  [the longest x1 19.5 us: step_call(): pl.pallas_call(functools.partial(step_kernel, sizes), out_shape=(vmem(gri...]
where the time goes in v1:
time: 27.2 us; the launch traced here: 27 us
  Pallas kernels  26.4 us (97%)
  between operations  0.64 us (2%)
    pallas_call x1, Pallas kernels, step_call(): pl.pallas_call(functools.partial(step_kernel, sizes), out_shape=(vmem(gri...  19.5 us
    pallas_call x1, Pallas kernels, force_call(): pl.pallas_call(force_kernel, out_shape=(jax.ShapeDtypeStruct(block, f32),...  6.93 us

profile of v1, /device:TPU:0, one launch (start us, length us, event | category | flops | bytes accessed | tf_op | source)
XLA Modules:
  0.0 27.0 jit_solution(9301150281860017138)
XLA Ops:
  0.6 19.5 %shard_map.67 = (f32[3,34,48,128]{3,2,1,0:T(8,128)S(1)}, f32[3,34,48,128]{3,2,1,0:T(8,128)S(1)}, f32[2,3,32,128]{3,2,1,0:T(8,128)S(1)}, f32[2,3,32,128]{3,2,1,0:...) custom-call(s32[3,16]{1,0:T(4,128)} %bitcast.5, ...), custom_call_target="tpu_custom_call" | custom-call | tf_op jit(solution)/shard_map/pallas_call | solution.py:517
  20.1 6.9 %shard_map.68 = (f32[3,32,32,128]{3,2,1,0:T(8,128)}, f32[256,256]{1,0:T(8,128)}, f32[256,256]{1,0:T(8,128)}) custom-call(s32[3,16]{1,0:T(4,128)} %bitcast.6, f32[3,34,48,128]{3,2,1,0:T(8,128)S(1)} %get-tuple-element.13.vel, f32[3,34,48,128]{3,2,1,0:T(8,128)S(1)} %get-tuple-element.14.pred, f32[2,3,32,128]{3,2,1,0:T(8,128)S(1)} %get-tuple-element.15.yrecv, ...), custom_call_target="tpu_custom_call" | custom-call | tf_op jit(solution)/shard_map/pallas_call | solution.py:622

commit v2 on v1

--- a/solution.py
+++ b/solution.py
@@ -21,8 +21,10 @@
 speck = 1.1e-19
 
 SUB = 8
-CHUNK = 8
+PLANES = 4
+EARLY = 1
 DEPOSIT = 4
+TURN = 12
 MIB = 1 << 20
 
 MESH = pl.DeviceIdType.MESH
@@ -93,7 +95,7 @@
             box.put(lev, i, g, 2.0 * jnp.concatenate(pieces, axis=0))
         return carry
 
-    lax.fori_loop(0, edge, fetch, 0, unroll=4)
+    lax.fori_loop(0, edge, fetch, 0, unroll=True)
 
 
 def window_matrix(box, corners):
@@ -130,7 +132,7 @@
                 mot[c, i, g] = acc
             return carry
 
-        lax.fori_loop(0, edge, gather, 0, unroll=2)
+        lax.fori_loop(0, edge, gather, 0, unroll=4)
 
 
 def lean(e1, e2, e3, e4):
@@ -224,10 +226,10 @@
             rate[i, g] = pseudo_step * out * lax.rsqrt(out * out + 1.0)
         return carry
 
-    lax.fori_loop(0, edge, advect, 0, unroll=2)
-
-
-def reinitialize(box, psa, psb, sign, rate):
+    lax.fori_loop(0, edge, advect, 0, unroll=8)
+
+
+def reinitialize(box, pairs, psa, psb, sign, rate):
     edge, here, below, above = box.edge, box.here, box.below, box.above
     low = jnp.where(box.k_first, 0.0, 1.0)
     high = jnp.where(box.k_last, 0.0, 1.0)
@@ -255,7 +257,7 @@
         sweep(psb, psa)
         return carry
 
-    lax.fori_loop(0, ITERS // 2, two_sweeps, 0)
+    lax.fori_loop(0, pairs, two_sweeps, 0)
 
 
 def curve_levels(box, owners, psi, nx, ny, part, force, native_a, native_b):
@@ -279,7 +281,7 @@
                 force[d, i, g] = c
         return carry
 
-    lax.fori_loop(0, edge, bend, 0, unroll=2)
+    lax.fori_loop(0, edge, bend, 0, unroll=8)
 
     alive = []
     for g in range(box.groups):
@@ -307,7 +309,7 @@
                 force[d, i, g] = force[d, i, g] * strength
         return carry
 
-    lax.fori_loop(0, edge, push, 0, unroll=2)
+    lax.fori_loop(0, edge, push, 0, unroll=8)
 
 
 class Grid:
@@ -347,55 +349,60 @@
                 pltpu.roll(zlow[c], 1, 1),
             )
 
-    def packed(self, value, x, acc):
-        return jnp.where(self.group == x, pltpu.roll(value, 4 * x + 1, 1), acc)
-
-    def shift(self, src, shifts, near, slot, first):
-        left = jnp.concatenate(
-            [halves(src[c, 1 + first + n, self.here]) for c in range(3) for n in range(CHUNK)], axis=0
-        )
-        both = jnp.dot(left, shifts[...], preferred_element_type=f32)
-        for c in range(3):
-            for n in range(CHUNK):
-                at = (c * CHUNK + n) * self.ys
-                for e in range(2):
-                    near[slot, c, n, e] = both[at : at + self.ys, e * self.lanes : (e + 1) * self.lanes]
-
-    def section(self, src, comb, shifts, near, scale, emit):
+    def pack(self, value, c, x, y, zsend):
+        tile = pl.ds(y, SUB)
+        turned = pltpu.roll(value, 4 * x + 1, 1)
+        zsend[c, tile] = jnp.where(self.group[:SUB] == x, turned, zsend[c, tile])
+
+    def shift(self, src, shifts, near):
+        span = self.xs // 2
+
+        def part(t, carry):
+            left = [halves(src[c, 1 + span * t + n, self.here]) for c in range(3) for n in range(span)]
+            both = jnp.dot(jnp.concatenate(left, axis=0), shifts[...], preferred_element_type=f32)
+            for c in range(3):
+                for n in range(span):
+                    at = (c * span + n) * self.ys
+                    for e in range(2):
+                        near[c, span * t + n, e] = both[at : at + self.ys, e * self.lanes : (e + 1) * self.lanes]
+            return carry
+
+        lax.fori_loop(0, 2, part, 0)
+
+    def section(self, src, comb, near, scale, emit):
         h = scale * grid_step * viscosity
-        chunks = self.xs // CHUNK
-
-        def chunk(t, carry):
-            slot = t % 2
-            self.shift(src, shifts, near, 1 - slot, CHUNK * jnp.minimum(t + 1, chunks - 1))
-            for n in range(CHUNK):
-                x = CHUNK * t + n
-                centre = [src[c, x + 1, self.here] for c in range(3)]
+        lane = self.lane[:SUB]
+        first, last = lane == 0, lane == self.lanes - 1
+
+        def plane(x, carry):
+            for y in range(0, self.ys, SUB):
+                rows, tile = pl.ds(SUB + y, SUB), pl.ds(y, SUB)
+                centre = [src[c, x + 1, rows] for c in range(3)]
                 w = [(0.5 * scale * grid_step) * v for v in centre]
                 up, down = [h - v for v in w], [h + v for v in w]
-                rim = jnp.where(self.lane == 0, down[2], jnp.where(self.lane == self.lanes - 1, up[2], 0.0))
+                rim = jnp.where(first, down[2], jnp.where(last, up[2], 0.0))
                 for c in range(3):
-                    halo = pltpu.roll(comb[c], self.lanes - 1 - 4 * x, 1)
+                    halo = pltpu.roll(comb[c, tile], self.lanes - 1 - 4 * x, 1)
                     value = (
                         (scale - 6.0 * h) * centre[c]
-                        + up[0] * src[c, x + 2, self.here]
-                        + down[0] * src[c, x, self.here]
-                        + up[1] * src[c, x + 1, self.above]
-                        + down[1] * src[c, x + 1, self.below]
-                        + up[2] * near[slot, c, n, 1]
-                        + down[2] * near[slot, c, n, 0]
+                        + up[0] * src[c, x + 2, rows]
+                        + down[0] * src[c, x, rows]
+                        + up[1] * src[c, x + 1, pl.ds(SUB + y + 1, SUB)]
+                        + down[1] * src[c, x + 1, pl.ds(SUB + y - 1, SUB)]
+                        + up[2] * near[c, x, 1, tile]
+                        + down[2] * near[c, x, 0, tile]
                         + rim * halo
                     )
-                    emit(c, x, value)
+                    emit(c, x, y, value)
             return carry
 
-        lax.fori_loop(0, chunks, chunk, 0)
+        lax.fori_loop(0, self.xs, plane, 0, unroll=PLANES)
 
 
 def step_kernel(
     sizes, corners, owners, v_hbm, lev_hbm,
-    vel, pred, yrecv1, zrecv1, force, native_a, native_b,
-    yrecv0, zrecv0, ysend, zsend, comb, near, shifts, windows, wide,
+    vel, pred, near1, yrecv1, zrecv1, force, native_a, native_b,
+    yrecv0, zrecv0, ysend, zsend, comb, near0, shifts, windows, wide,
     native, lev, mi, di, mj, dj, mot, psa, psb, sign, rate,
     local_sem, lev_sem, send_sem, recv_sem,
 ):
@@ -405,14 +412,15 @@
     edge = lev.shape[0]
     box = Box(edge, lanes, slots)
     inner = pl.ds(1, xs)
+    loads = [
+        pltpu.make_async_copy(v_hbm.at[c], vel.at[c, inner, grid.here], local_sem.at[c]) for c in range(3)
+    ]
     levels = [
         pltpu.make_async_copy(lev_hbm.at[:, pl.ds(h * lanes, lanes)], native.at[h], lev_sem.at[h])
         for h in range(box.halves)
     ]
-    for part in levels:
+    for part in loads + levels:
         part.start()
-    load = pltpu.make_async_copy(v_hbm, vel.at[:, inner, grid.here], local_sem)
-    load.start()
     ups, downs = [], []
     for axis in ("gx", "gy", "gz"):
         me, n = lax.axis_index(axis), sizes[axis]
@@ -423,10 +431,6 @@
         pl.semaphore_signal(barrier, inc=1, device_id=target, device_id_type=MESH)
     shifts[...] = shift_matrix(lanes)
     windows[...] = window_matrix(box, corners)
-    for part in levels:
-        part.wait()
-    fetch_levels(box, native, lev)
-    load.wait()
 
     def exchange(r, src, yrecv, zrecv):
         copies = []
@@ -451,21 +455,20 @@
         send(5, zsend.at[r], zrecv.at[1], downs[2])
         return copies
 
+    group = grid.group
     for c in range(3):
-        zsend[0, c] = jnp.zeros((ys, lanes), f32)
+        loads[c].wait()
+
+        def pack(x, acc, c=c):
+            return jnp.where(group == x, pltpu.roll(vel[c, x + 1, grid.here], 4 * x + 1, 1), acc)
+
+        zsend[0, c] = lax.fori_loop(0, xs, pack, jnp.zeros((ys, lanes), f32), unroll=8)
         zsend[1, c] = jnp.zeros((ys, lanes), f32)
+    grid.take_rows(vel, ysend.at[0])
     span = xs // 2
 
     def spread(t, carry):
-        left = []
-        for c in range(3):
-            acc = zsend[0, c]
-            for n in range(span):
-                x = span * t + n
-                value = vel[c, x + 1, grid.here]
-                left.append(halves(value))
-                acc = grid.packed(value, x, acc)
-            zsend[0, c] = acc
+        left = [halves(vel[c, span * t + n + 1, grid.here]) for c in range(3) for n in range(span)]
         both = jnp.dot(jnp.concatenate(left, axis=0), windows[...], preferred_element_type=f32)
         for c in range(3):
             for n in range(span):
@@ -474,26 +477,30 @@
                     wide[c, g, span * t + n] = both[at : at + ys, g * lanes : (g + 1) * lanes]
         return carry
 
-    lax.fori_loop(0, xs // span, spread, 0)
-    grid.take_rows(vel, ysend.at[0])
     pl.semaphore_wait(barrier, 6)
     copies = exchange(0, vel, yrecv0, zrecv0)
+    lax.fori_loop(0, xs // span, spread, 0)
+    for part in levels:
+        part.wait()
+    fetch_levels(box, native, lev)
     gather_motion(box, corners, wide, mot)
     advect_levels(box, lev, mi, di, mj, dj, mot, psa, sign, rate)
-    grid.shift(vel, shifts, near, 0, 0)
+    grid.shift(vel, shifts, near0)
+    reinitialize(box, EARLY, psa, psb, sign, rate)
     for copy in copies:
         copy.wait()
     grid.fill_rows(vel, yrecv0.at[0], yrecv0.at[1])
     grid.combine(zrecv0.at[0], zrecv0.at[1], comb)
 
-    def first(c, x, value):
-        pred[c, x + 1, grid.here] = value
-        zsend[1, c] = grid.packed(value, x, zsend[1, c])
-
-    grid.section(vel, comb, shifts, near, 1.0, first)
+    def first(c, x, y, value):
+        pred[c, x + 1, pl.ds(SUB + y, SUB)] = value
+        grid.pack(value, c, x, y, zsend.at[1])
+
+    grid.section(vel, comb, near0, 1.0, first)
     grid.take_rows(pred, ysend.at[1])
     copies = exchange(1, pred, yrecv1, zrecv1)
-    reinitialize(box, psa, psb, sign, rate)
+    grid.shift(pred, shifts, near1)
+    reinitialize(box, ITERS // 2 - EARLY, psa, psb, sign, rate)
     curve_levels(box, owners, psa, mi, mj, di, force, native_a, native_b)
     for copy in copies:
         copy.wait()
@@ -519,6 +526,7 @@
         out_shape=(
             vmem(grid_shape, f32),
             vmem(grid_shape, f32),
+            vmem((3, xs, 2, ys, lanes), f32),
             vmem((2, 3, xs, lanes), f32),
             vmem((2, 3, ys, lanes), f32),
             vmem((3,) + flat, f32),
@@ -526,14 +534,14 @@
             vmem(native, f32),
         ),
         in_specs=[smem, smem, pl.BlockSpec(memory_space=pltpu.HBM), pl.BlockSpec(memory_space=pltpu.HBM)],
-        out_specs=(pl.BlockSpec(memory_space=vmem),) * 7,
+        out_specs=(pl.BlockSpec(memory_space=vmem),) * 8,
         scratch_shapes=[
             vmem((2, 3, xs, lanes), f32),
             vmem((2, 3, ys, lanes), f32),
             vmem((2, 2, 3, xs, lanes), f32),
             vmem((2, 3, ys, lanes), f32),
             vmem((3, ys, lanes), f32),
-            vmem((2, 3, CHUNK, 2, ys, lanes), f32),
+            vmem((3, xs, 2, ys, lanes), f32),
             vmem((2 * lanes, 2 * lanes), bf16),
             vmem((2 * lanes, groups * lanes), bf16),
             vmem((3, groups, xs, ys, lanes), f32),
@@ -548,7 +556,7 @@
             vmem(tall, f32),
             vmem(flat, f32),
             vmem(flat, f32),
-            pltpu.SemaphoreType.DMA(()),
+            pltpu.SemaphoreType.DMA((3,)),
             pltpu.SemaphoreType.DMA((plane // lanes,)),
             pltpu.SemaphoreType.DMA((2, 6)),
             pltpu.SemaphoreType.DMA((2, 6)),
@@ -560,9 +568,9 @@
 
 
 def force_kernel(
-    corners, vel, pred, yrecv, zrecv, force, native_a, native_b,
+    corners, vel, pred, near, yrecv, zrecv, force, native_a, native_b,
     o_hbm, set_hbm, ben_hbm,
-    src, o_ref, comb, near, shifts, out_sem, small_sem,
+    o_ref, comb, place, out_sem, small_sem,
 ):
     _, xs, ys, lanes = o_ref.shape
     grid = Grid(xs, ys, lanes)
@@ -577,34 +585,60 @@
         stores.append(pltpu.make_async_copy(native_b.at[h], ben_hbm.at[:, part_h], small_sem.at[1, h]))
     for copy in stores:
         copy.start()
-    shifts[...] = shift_matrix(lanes)
     grid.combine(zrecv.at[0], zrecv.at[1], comb)
-    grid.shift(pred, shifts, near, 0, 0)
-
-    def second(c, x, value):
-        o_ref[c, x] = 0.5 * vel[c, x + 1, grid.here] + value
+
+    def second(c, x, y, value):
+        o_ref[c, x, pl.ds(y, SUB)] = 0.5 * vel[c, x + 1, pl.ds(SUB + y, SUB)] + value
 
     grid.fill_rows(pred, yrecv.at[0], yrecv.at[1])
-    grid.section(pred, comb, shifts, near, 0.5, second)
+    grid.section(pred, comb, near, 0.5, second)
 
     wide = iota((edge, lanes), 1)
 
-    def deposit_slot(n, carry):
-        g, s = n // per, n % per
+    offset = iota((edge, lanes), 1) - iota((edge, lanes), 0)
+    spots = [(c, i) for c in range(3) for i in range(edge)]
+
+    def turned(n, force_at):
         ax, ay, az = corners[0, n], corners[1, n], corners[2, n]
-        turn = lax.rem(az + lanes - s * edge, lanes)
+        turn = lax.rem(az + lanes - n % per * edge, lanes)
         inside = jnp.logical_and(wide >= az, wide < az + edge)
-
-        for i in range(0, edge, DEPOSIT):
-            spots = [(c, i + t) for t in range(DEPOSIT) for c in range(3)]
-            blocks = [pltpu.roll(force[c, q, g], turn, 1) for c, q in spots]
-            olds = [o_ref[c, ax + q, pl.ds(ay, edge), :] for c, q in spots]
-            news = [old + jnp.where(inside, block, 0.0) for old, block in zip(olds, blocks)]
-            for (c, q), new in zip(spots, news):
-                o_ref[c, ax + q, pl.ds(ay, edge), :] = new
-        return carry
-
-    lax.fori_loop(0, slots, deposit_slot, 0)
+        for at in range(0, len(spots), TURN):
+            some = spots[at : at + TURN]
+            blocks = [pltpu.roll(force_at(c, i), turn, 1) for c, i in some]
+            olds = [o_ref[c, ax + i, pl.ds(ay, edge), :] for c, i in some]
+            for (c, i), old, block in zip(some, olds, blocks):
+                o_ref[c, ax + i, pl.ds(ay, edge), :] = old + jnp.where(inside, block, 0.0)
+
+    def deposit(t, carry):
+        base = t * DEPOSIT
+        g = base // per
+
+        def force_at(c, i):
+            return force[c, i, g]
+
+        for e in range(2):
+            slot = base + e
+            mark = ones(offset == corners[2, slot])
+            blank = jnp.zeros_like(mark)
+            for r in range(per):
+                value = jnp.where(slot % per == r, mark, blank)
+                for part in range(2):
+                    place[pl.ds(part * lanes + r * edge, edge), e * lanes : (e + 1) * lanes] = value
+        left = jnp.concatenate([halves(force_at(c, i)) for c, i in spots], axis=0)
+        both = jnp.dot(left, place[...], preferred_element_type=f32)
+        for e in range(2, DEPOSIT):
+            turned(base + e, force_at)
+        for e in range(2):
+            ax, ay = corners[0, base + e], corners[1, base + e]
+            for n, (c, i) in enumerate(spots):
+                rows = pl.ds(ay, edge)
+                o_ref[c, ax + i, rows, :] = (
+                    o_ref[c, ax + i, rows, :]
+                    + both[n * edge : (n + 1) * edge, e * lanes : (e + 1) * lanes]
+                )
+        return carry
+
+    lax.fori_loop(0, slots // DEPOSIT, deposit, 0)
     for c in range(3):
         stores.append(pltpu.make_async_copy(o_ref.at[c], o_hbm.at[c], out_sem.at[c]))
         stores[-1].start()
@@ -626,13 +660,11 @@
             jax.ShapeDtypeStruct(flat, f32),
             jax.ShapeDtypeStruct(flat, f32),
         ),
-        in_specs=[smem] + [whole] * 7,
+        in_specs=[smem] + [whole] * 8,
         out_specs=(pl.BlockSpec(memory_space=pltpu.HBM),) * 3,
         scratch_shapes=[
-            pltpu.VMEM((SUB, lanes), f32),
             pltpu.VMEM(block, f32),
             pltpu.VMEM((3, ys, lanes), f32),
-            pltpu.VMEM((2, 3, CHUNK, 2, ys, lanes), f32),
             pltpu.VMEM((2 * lanes, 2 * lanes), bf16),
             pltpu.SemaphoreType.DMA((3,)),
             pltpu.SemaphoreType.DMA((2, plane // lanes)),

time: 27.2 us -> 22.7 us (0.83)
  Pallas kernels: 26.4 us -> 21.9 us
    pallas_call x1, Pallas kernels: 19.5 us -> 17 us  [step_call(): pl.pallas_call(functools.partial(step_kernel, sizes), out_shape=(vmem(gri...]
    pallas_call x1, Pallas kernels: 6.93 us -> 4.85 us  [force_call(): pl.pallas_call(force_kernel, out_shape=(jax.ShapeDtypeStruct(block, f32),...]
where the time goes in v2:
time: 22.7 us; the launch traced here: 22.5 us
  Pallas kernels  21.9 us (96%)
  between operations  0.64 us (3%)
    pallas_call x1, Pallas kernels, step_call(): pl.pallas_call(functools.partial(step_kernel, sizes), out_shape=(vmem(gri...  17 us
    pallas_call x1, Pallas kernels, force_call(): pl.pallas_call(force_kernel, out_shape=(jax.ShapeDtypeStruct(block, f32),...  4.85 us

profile of v2, /device:TPU:0, one launch (start us, length us, event | category | flops | bytes accessed | tf_op | source)
XLA Modules:
  0.0 22.5 jit_solution(9000578192542093660)
XLA Ops:
  0.6 17.0 %shard_map.67 = (f32[3,34,48,128]{3,2,1,0:T(8,128)S(1)}, f32[3,34,48,128]{3,2,1,0:T(8,128)S(1)}, f32[3,32,2,32,128]{4,3,2,1,0:T(8,128)S(1)}, f32[2,3,32,128]{3,2...) custom-call(s32[3,16]{1,0:T(4,128)} %bitcast.5, ...), custom_call_target="tpu_custom_call" | custom-call | tf_op jit(solution)/shard_map/pallas_call | solution.py:524
  17.6 4.9 %shard_map.68 = (f32[3,32,32,128]{3,2,1,0:T(8,128)}, f32[256,256]{1,0:T(8,128)}, f32[256,256]{1,0:T(8,128)}) custom-call(s32[3,16]{1,0:T(4,128)} %bitcast.6, f32[3,34,48,128]{3,2,1,0:T(8,128)S(1)} %get-tuple-element.14.vel, f32[3,34,48,128]{3,2,1,0:T(8,128)S(1)} %get-tuple-element.15.pred, f32[3,32,2,32,128]{4,3,2,1,0:T(8,128)S(1)} %get-tuple-element.16.near, ...), custom_call_target="tpu_custom_call" | custom-call | tf_op jit(solution)/shard_map/pallas_call | solution.py:656

commit v3 on v2

--- a/solution.py
+++ b/solution.py
@@ -21,7 +21,8 @@
 speck = 1.1e-19
 
 SUB = 8
-PLANES = 4
+PLANES = 6
+FUSE = 4
 EARLY = 1
 DEPOSIT = 4
 TURN = 12
@@ -83,19 +84,16 @@
         ref[i, g, last : last + 1] = value[self.edge - 1 :]
 
 
-def fetch_levels(box, native, lev):
+def fetch_levels(box, native, lev, first, count):
     edge, per = box.edge, box.per
-
-    def fetch(i, carry):
+    for n in range(count):
+        i = first + n
         for g in range(box.groups):
             pieces = [
                 box.swap_blocks(native[h, pl.ds(g * per * edge + i, per, stride=edge), :])
                 for h in range(box.halves)
             ]
             box.put(lev, i, g, 2.0 * jnp.concatenate(pieces, axis=0))
-        return carry
-
-    lax.fori_loop(0, edge, fetch, 0, unroll=True)
 
 
 def window_matrix(box, corners):
@@ -119,20 +117,23 @@
 
 
 def gather_motion(box, corners, wide, mot):
-    edge, per = box.edge, box.per
-    for g in range(box.groups):
-        places = [[corners[d, g * per + s] for d in range(2)] for s in range(per)]
-
-        def gather(i, carry, g=g, places=places):
-            for c in range(3):
-                acc = None
-                for s in range(per):
-                    rows = wide[c, g, places[s][0] + i, pl.ds(places[s][1], edge), :]
-                    acc = rows if acc is None else jnp.where(box.block == s, rows, acc)
-                mot[c, i, g] = acc
-            return carry
-
-        lax.fori_loop(0, edge, gather, 0, unroll=4)
+    edge = box.edge
+    slots = box.per * box.groups
+    places = [[corners[d, n] for d in range(2)] for n in range(slots)]
+
+    def gather(first, count):
+        for n in range(count):
+            i = first + n
+            for g in range(box.groups):
+                for c in range(3):
+                    acc = None
+                    for s in range(box.per):
+                        ax, ay = places[g * box.per + s]
+                        rows = wide[c, g, ax + i, pl.ds(ay, edge), :]
+                        acc = rows if acc is None else jnp.where(box.block == s, rows, acc)
+                    mot[c, i, g] = acc
+
+    return gather
 
 
 def lean(e1, e2, e3, e4):
@@ -229,7 +230,7 @@
     lax.fori_loop(0, edge, advect, 0, unroll=8)
 
 
-def reinitialize(box, pairs, psa, psb, sign, rate):
+def reinitialize(box, psa, psb, sign, rate):
     edge, here, below, above = box.edge, box.here, box.below, box.above
     low = jnp.where(box.k_first, 0.0, 1.0)
     high = jnp.where(box.k_last, 0.0, 1.0)
@@ -257,7 +258,13 @@
         sweep(psb, psa)
         return carry
 
-    lax.fori_loop(0, pairs, two_sweeps, 0)
+    def run(pairs):
+        if pairs == 1:
+            two_sweeps(0, 0)
+        else:
+            lax.fori_loop(0, pairs, two_sweeps, 0)
+
+    return run
 
 
 def curve_levels(box, owners, psi, nx, ny, part, force, native_a, native_b):
@@ -321,7 +328,6 @@
         self.rows = ys + 2 * SUB
         self.shape = (3, xs + 2, self.rows, lanes)
         self.lane = iota((ys, lanes), 1)
-        self.group = self.lane // 4
 
     def row_of(self, ref, c, x, row):
         flat = ref.reshape(3 * (self.xs + 2) * self.rows, self.lanes)
@@ -342,20 +348,17 @@
                 ysend[1, c, part] = self.row_of(ref, c, x + 1, SUB)[...]
 
     def combine(self, zlow, zhigh, comb):
+        high = pltpu.roll(zhigh[...], self.lanes - 2, 1)
         for c in range(3):
-            comb[c] = jnp.where(
-                self.lane % 4 == 0,
-                pltpu.roll(zhigh[c], self.lanes - 1, 1),
-                pltpu.roll(zlow[c], 1, 1),
-            )
-
-    def pack(self, value, c, x, y, zsend):
-        tile = pl.ds(y, SUB)
-        turned = pltpu.roll(value, 4 * x + 1, 1)
-        zsend[c, tile] = jnp.where(self.group[:SUB] == x, turned, zsend[c, tile])
-
-    def shift(self, src, shifts, near):
-        span = self.xs // 2
+            comb[c] = jnp.where(self.lane % 4 == c, zlow[...], high)
+
+    def pack(self, value, c, x, faces):
+        lane = self.lane[: value.shape[0]] - 4 * x
+        turned = pltpu.roll(value, 4 * x + c + 1, 1)
+        return jnp.where(lane == c, turned, faces[0]), jnp.where(lane == c + 1, turned, faces[1])
+
+    def shift(self, src, shifts, near, pieces, also):
+        span = self.xs // pieces
 
         def part(t, carry):
             left = [halves(src[c, 1 + span * t + n, self.here]) for c in range(3) for n in range(span)]
@@ -365,11 +368,12 @@
                     at = (c * span + n) * self.ys
                     for e in range(2):
                         near[c, span * t + n, e] = both[at : at + self.ys, e * self.lanes : (e + 1) * self.lanes]
+            also(t)
             return carry
 
-        lax.fori_loop(0, 2, part, 0)
-
-    def section(self, src, comb, near, scale, emit):
+        lax.fori_loop(0, pieces, part, 0)
+
+    def section(self, src, comb, near, scale, emit, ends_done, unroll):
         h = scale * grid_step * viscosity
         lane = self.lane[:SUB]
         first, last = lane == 0, lane == self.lanes - 1
@@ -381,9 +385,11 @@
                 w = [(0.5 * scale * grid_step) * v for v in centre]
                 up, down = [h - v for v in w], [h + v for v in w]
                 rim = jnp.where(first, down[2], jnp.where(last, up[2], 0.0))
+                values = []
                 for c in range(3):
-                    halo = pltpu.roll(comb[c, tile], self.lanes - 1 - 4 * x, 1)
-                    value = (
+                    turn = lax.rem(2 * self.lanes - c - 4 * x, self.lanes)
+                    halo = pltpu.roll(comb[c, tile], turn, 1)
+                    values.append(
                         (scale - 6.0 * h) * centre[c]
                         + up[0] * src[c, x + 2, rows]
                         + down[0] * src[c, x, rows]
@@ -393,10 +399,16 @@
                         + down[2] * near[c, x, 0, tile]
                         + rim * halo
                     )
-                    emit(c, x, y, value)
+                emit(x, y, values)
             return carry
 
-        lax.fori_loop(0, self.xs, plane, 0, unroll=PLANES)
+        if ends_done is None:
+            lax.fori_loop(0, self.xs, plane, 0, unroll=unroll)
+            return
+        plane(0, 0)
+        plane(self.xs - 1, 0)
+        ends_done()
+        lax.fori_loop(1, self.xs - 1, plane, 0, unroll=unroll)
 
 
 def step_kernel(
@@ -432,39 +444,47 @@
     shifts[...] = shift_matrix(lanes)
     windows[...] = window_matrix(box, corners)
 
-    def exchange(r, src, yrecv, zrecv):
-        copies = []
-
-        def send(n, src, dst, target):
-            copy = pltpu.make_async_remote_copy(
-                src_ref=src,
-                dst_ref=dst,
-                send_sem=send_sem.at[r, n],
-                recv_sem=recv_sem.at[r, n],
-                device_id=target,
-                device_id_type=MESH,
-            )
-            copy.start()
-            copies.append(copy)
-
-        send(0, src.at[:, xs, grid.here], src.at[:, 0, grid.here], ups[0])
-        send(1, src.at[:, 1, grid.here], src.at[:, xs + 1, grid.here], downs[0])
-        send(2, ysend.at[r, 0], yrecv.at[0], ups[1])
-        send(3, ysend.at[r, 1], yrecv.at[1], downs[1])
-        send(4, zsend.at[r], zrecv.at[0], ups[2])
-        send(5, zsend.at[r], zrecv.at[1], downs[2])
-        return copies
-
-    group = grid.group
+    copies = [[], []]
+
+    def send(r, n, src, dst, target):
+        copy = pltpu.make_async_remote_copy(
+            src_ref=src,
+            dst_ref=dst,
+            send_sem=send_sem.at[r, n],
+            recv_sem=recv_sem.at[r, n],
+            device_id=target,
+            device_id_type=MESH,
+        )
+        copy.start()
+        copies[r].append(copy)
+
+    def send_x(r, src):
+        send(r, 0, src.at[:, xs, grid.here], src.at[:, 0, grid.here], ups[0])
+        send(r, 1, src.at[:, 1, grid.here], src.at[:, xs + 1, grid.here], downs[0])
+
+    def send_yz(r, yrecv, zrecv):
+        send(r, 2, ysend.at[r, 0], yrecv.at[0], ups[1])
+        send(r, 3, ysend.at[r, 1], yrecv.at[1], downs[1])
+        send(r, 4, zsend.at[r, 0], zrecv.at[0], ups[2])
+        send(r, 5, zsend.at[r, 1], zrecv.at[1], downs[2])
+
+    blank = jnp.zeros((ys, lanes), f32)
+    faces = blank, blank
     for c in range(3):
         loads[c].wait()
 
-        def pack(x, acc, c=c):
-            return jnp.where(group == x, pltpu.roll(vel[c, x + 1, grid.here], 4 * x + 1, 1), acc)
-
-        zsend[0, c] = lax.fori_loop(0, xs, pack, jnp.zeros((ys, lanes), f32), unroll=8)
-        zsend[1, c] = jnp.zeros((ys, lanes), f32)
+        def pack(x, faces, c=c):
+            return grid.pack(vel[c, x + 1, grid.here], c, x, faces)
+
+        faces = lax.fori_loop(0, xs, pack, faces, unroll=8)
+    zsend[0, 0], zsend[0, 1] = faces
+    zsend[1, 0], zsend[1, 1] = blank, blank
     grid.take_rows(vel, ysend.at[0])
+    pl.semaphore_wait(barrier, 6)
+    send_x(0, vel)
+    send_yz(0, yrecv0, zrecv0)
+    for part in levels:
+        part.wait()
     span = xs // 2
 
     def spread(t, carry):
@@ -475,34 +495,38 @@
                 at = (c * span + n) * ys
                 for g in range(box.groups):
                     wide[c, g, span * t + n] = both[at : at + ys, g * lanes : (g + 1) * lanes]
+        fetch_levels(box, native, lev, t * (edge // 2), edge // 2)
         return carry
 
-    pl.semaphore_wait(barrier, 6)
-    copies = exchange(0, vel, yrecv0, zrecv0)
-    lax.fori_loop(0, xs // span, spread, 0)
-    for part in levels:
-        part.wait()
-    fetch_levels(box, native, lev)
-    gather_motion(box, corners, wide, mot)
+    lax.fori_loop(0, 2, spread, 0)
+    gather = gather_motion(box, corners, wide, mot)
+    grid.shift(vel, shifts, near0, 2, lambda t: gather(t * (edge // 2), edge // 2))
     advect_levels(box, lev, mi, di, mj, dj, mot, psa, sign, rate)
-    grid.shift(vel, shifts, near0)
-    reinitialize(box, EARLY, psa, psb, sign, rate)
-    for copy in copies:
+    reinitialize(box, psa, psb, sign, rate)(EARLY)
+    for copy in copies[0]:
         copy.wait()
     grid.fill_rows(vel, yrecv0.at[0], yrecv0.at[1])
     grid.combine(zrecv0.at[0], zrecv0.at[1], comb)
 
-    def first(c, x, y, value):
-        pred[c, x + 1, pl.ds(SUB + y, SUB)] = value
-        grid.pack(value, c, x, y, zsend.at[1])
-
-    grid.section(vel, comb, near0, 1.0, first)
+    def first(x, y, values):
+        tile = pl.ds(y, SUB)
+        faces = zsend[1, 0, tile], zsend[1, 1, tile]
+        for c, value in enumerate(values):
+            pred[c, x + 1, pl.ds(SUB + y, SUB)] = value
+            faces = grid.pack(value, c, x, faces)
+        zsend[1, 0, tile], zsend[1, 1, tile] = faces
+
+    grid.section(vel, comb, near0, 1.0, first, lambda: send_x(1, pred), PLANES)
     grid.take_rows(pred, ysend.at[1])
-    copies = exchange(1, pred, yrecv1, zrecv1)
-    grid.shift(pred, shifts, near1)
-    reinitialize(box, ITERS // 2 - EARLY, psa, psb, sign, rate)
+    send_yz(1, yrecv1, zrecv1)
+    two_sweeps = reinitialize(box, psa, psb, sign, rate)
+    if FUSE:
+        grid.shift(pred, shifts, near1, FUSE, lambda t: two_sweeps(1))
+    else:
+        grid.shift(pred, shifts, near1, 2, lambda t: None)
+    two_sweeps(ITERS // 2 - EARLY - FUSE)
     curve_levels(box, owners, psa, mi, mj, di, force, native_a, native_b)
-    for copy in copies:
+    for copy in copies[1]:
         copy.wait()
 
 
@@ -528,7 +552,7 @@
             vmem(grid_shape, f32),
             vmem((3, xs, 2, ys, lanes), f32),
             vmem((2, 3, xs, lanes), f32),
-            vmem((2, 3, ys, lanes), f32),
+            vmem((2, ys, lanes), f32),
             vmem((3,) + flat, f32),
             vmem(native, f32),
             vmem(native, f32),
@@ -537,9 +561,9 @@
         out_specs=(pl.BlockSpec(memory_space=vmem),) * 8,
         scratch_shapes=[
             vmem((2, 3, xs, lanes), f32),
-            vmem((2, 3, ys, lanes), f32),
+            vmem((2, ys, lanes), f32),
             vmem((2, 2, 3, xs, lanes), f32),
-            vmem((2, 3, ys, lanes), f32),
+            vmem((2, 2, ys, lanes), f32),
             vmem((3, ys, lanes), f32),
             vmem((3, xs, 2, ys, lanes), f32),
             vmem((2 * lanes, 2 * lanes), bf16),
@@ -587,11 +611,12 @@
         copy.start()
     grid.combine(zrecv.at[0], zrecv.at[1], comb)
 
-    def second(c, x, y, value):
-        o_ref[c, x, pl.ds(y, SUB)] = 0.5 * vel[c, x + 1, pl.ds(SUB + y, SUB)] + value
+    def second(x, y, values):
+        for c, value in enumerate(values):
+            o_ref[c, x, pl.ds(y, SUB)] = 0.5 * vel[c, x + 1, pl.ds(SUB + y, SUB)] + value
 
     grid.fill_rows(pred, yrecv.at[0], yrecv.at[1])
-    grid.section(pred, comb, near, 0.5, second)
+    grid.section(pred, comb, near, 0.5, second, None, 8)
 
     wide = iota((edge, lanes), 1)
 

time: 22.7 us -> 22 us (0.969)
  Pallas kernels: 21.9 us -> 21.2 us
    pallas_call x1, Pallas kernels: 17 us -> 16.3 us  [step_call(): pl.pallas_call(functools.partial(step_kernel, sizes), out_shape=(vmem(gri...]
where the time goes in v3:
time: 22 us; the launch traced here: 21.8 us
  Pallas kernels  21.2 us (96%)
  between operations  0.64 us (3%)
    pallas_call x1, Pallas kernels, step_call(): pl.pallas_call(functools.partial(step_kernel, sizes), out_shape=(vmem(gri...  16.3 us
    pallas_call x1, Pallas kernels, force_call(): pl.pallas_call(force_kernel, out_shape=(jax.ShapeDtypeStruct(block, f32),...  4.9 us

profile of v3, /device:TPU:0, one launch (start us, length us, event | category | flops | bytes accessed | tf_op | source)
XLA Modules:
  0.0 21.8 jit_solution(15822679139542536350)
XLA Ops:
  0.6 16.3 %shard_map.67 = (f32[3,34,48,128]{3,2,1,0:T(8,128)S(1)}, f32[3,34,48,128]{3,2,1,0:T(8,128)S(1)}, f32[3,32,2,32,128]{4,3,2,1,0:T(8,128)S(1)}, f32[2,3,32,128]{3,2...) custom-call(s32[3,16]{1,0:T(4,128)} %bitcast.5, ...), custom_call_target="tpu_custom_call" | custom-call | tf_op jit(solution)/shard_map/pallas_call | solution.py:548
  16.9 4.9 %shard_map.68 = (f32[3,32,32,128]{3,2,1,0:T(8,128)}, f32[256,256]{1,0:T(8,128)}, f32[256,256]{1,0:T(8,128)}) custom-call(s32[3,16]{1,0:T(4,128)} %bitcast.6, f32[3,34,48,128]{3,2,1,0:T(8,128)S(1)} %get-tuple-element.14.vel, f32[3,34,48,128]{3,2,1,0:T(8,128)S(1)} %get-tuple-element.15.pred, f32[3,32,2,32,128]{4,3,2,1,0:T(8,128)S(1)} %get-tuple-element.16.near, ...), custom_call_target="tpu_custom_call" | custom-call | tf_op jit(solution)/shard_map/pallas_call | solution.py:681

commit v4 on v3

--- a/solution.py
+++ b/solution.py
@@ -22,8 +22,8 @@
 
 SUB = 8
 PLANES = 6
-FUSE = 4
-EARLY = 1
+FUSE = 2
+AHEAD = (1, 2, 3)
 DEPOSIT = 4
 TURN = 12
 MIB = 1 << 20
@@ -259,7 +259,7 @@
         return carry
 
     def run(pairs):
-        if pairs == 1:
+        if isinstance(pairs, int) and pairs == 1:
             two_sweeps(0, 0)
         else:
             lax.fori_loop(0, pairs, two_sweeps, 0)
@@ -444,29 +444,38 @@
     shifts[...] = shift_matrix(lanes)
     windows[...] = window_matrix(box, corners)
 
-    copies = [[], []]
-
-    def send(r, n, src, dst, target):
-        copy = pltpu.make_async_remote_copy(
-            src_ref=src,
-            dst_ref=dst,
-            send_sem=send_sem.at[r, n],
-            recv_sem=recv_sem.at[r, n],
-            device_id=target,
-            device_id_type=MESH,
-        )
-        copy.start()
-        copies[r].append(copy)
-
-    def send_x(r, src):
-        send(r, 0, src.at[:, xs, grid.here], src.at[:, 0, grid.here], ups[0])
-        send(r, 1, src.at[:, 1, grid.here], src.at[:, xs + 1, grid.here], downs[0])
-
-    def send_yz(r, yrecv, zrecv):
-        send(r, 2, ysend.at[r, 0], yrecv.at[0], ups[1])
-        send(r, 3, ysend.at[r, 1], yrecv.at[1], downs[1])
-        send(r, 4, zsend.at[r, 0], zrecv.at[0], ups[2])
-        send(r, 5, zsend.at[r, 1], zrecv.at[1], downs[2])
+    def exchange(r, src, yrecv, zrecv):
+        def copy(n, src, dst, target):
+            return pltpu.make_async_remote_copy(
+                src_ref=src,
+                dst_ref=dst,
+                send_sem=send_sem.at[r, n],
+                recv_sem=recv_sem.at[r, n],
+                device_id=target,
+                device_id_type=MESH,
+            )
+
+        return [
+            copy(0, src.at[:, xs, grid.here], src.at[:, 0, grid.here], ups[0]),
+            copy(1, src.at[:, 1, grid.here], src.at[:, xs + 1, grid.here], downs[0]),
+            copy(2, ysend.at[r, 0], yrecv.at[0], ups[1]),
+            copy(3, ysend.at[r, 1], yrecv.at[1], downs[1]),
+            copy(4, zsend.at[r, 0], zrecv.at[0], ups[2]),
+            copy(5, zsend.at[r, 1], zrecv.at[1], downs[2]),
+        ]
+
+    copies = exchange(0, vel, yrecv0, zrecv0), exchange(1, pred, yrecv1, zrecv1)
+
+    at = [lax.axis_index(axis) for axis in ("gx", "gy", "gz")]
+    low = at[2] == 0
+    first_in = jnp.logical_and(low, jnp.logical_and(at[0] == 0, at[1] < 2))
+
+    def send_blocks(when):
+        @pl.when(when)
+        def _():
+            pl.semaphore_wait(barrier, 6)
+            for copy in copies[0][4:] + copies[0][:4]:
+                copy.start()
 
     blank = jnp.zeros((ys, lanes), f32)
     faces = blank, blank
@@ -476,13 +485,11 @@
         def pack(x, faces, c=c):
             return grid.pack(vel[c, x + 1, grid.here], c, x, faces)
 
-        faces = lax.fori_loop(0, xs, pack, faces, unroll=8)
+        faces = lax.fori_loop(0, xs, pack, faces, unroll=True)
     zsend[0, 0], zsend[0, 1] = faces
     zsend[1, 0], zsend[1, 1] = blank, blank
     grid.take_rows(vel, ysend.at[0])
-    pl.semaphore_wait(barrier, 6)
-    send_x(0, vel)
-    send_yz(0, yrecv0, zrecv0)
+    send_blocks(jnp.logical_not(first_in))
     for part in levels:
         part.wait()
     span = xs // 2
@@ -501,8 +508,11 @@
     lax.fori_loop(0, 2, spread, 0)
     gather = gather_motion(box, corners, wide, mot)
     grid.shift(vel, shifts, near0, 2, lambda t: gather(t * (edge // 2), edge // 2))
+    send_blocks(first_in)
     advect_levels(box, lev, mi, di, mj, dj, mot, psa, sign, rate)
-    reinitialize(box, psa, psb, sign, rate)(EARLY)
+    two_sweeps = reinitialize(box, psa, psb, sign, rate)
+    ahead = jnp.where(first_in, AHEAD[2], jnp.where(low, AHEAD[1], AHEAD[0]))
+    two_sweeps(ahead)
     for copy in copies[0]:
         copy.wait()
     grid.fill_rows(vel, yrecv0.at[0], yrecv0.at[1])
@@ -516,15 +526,14 @@
             faces = grid.pack(value, c, x, faces)
         zsend[1, 0, tile], zsend[1, 1, tile] = faces
 
-    grid.section(vel, comb, near0, 1.0, first, lambda: send_x(1, pred), PLANES)
+    grid.section(vel, comb, near0, 1.0, first, lambda: [copy.start() for copy in copies[1][:2]], PLANES)
+    for copy in copies[1][4:]:
+        copy.start()
     grid.take_rows(pred, ysend.at[1])
-    send_yz(1, yrecv1, zrecv1)
-    two_sweeps = reinitialize(box, psa, psb, sign, rate)
-    if FUSE:
-        grid.shift(pred, shifts, near1, FUSE, lambda t: two_sweeps(1))
-    else:
-        grid.shift(pred, shifts, near1, 2, lambda t: None)
-    two_sweeps(ITERS // 2 - EARLY - FUSE)
+    for copy in copies[1][2:4]:
+        copy.start()
+    grid.shift(pred, shifts, near1, FUSE, lambda t: two_sweeps(1))
+    two_sweeps(ITERS // 2 - FUSE - ahead)
     curve_levels(box, owners, psa, mi, mj, di, force, native_a, native_b)
     for copy in copies[1]:
         copy.wait()

time: 22 us -> 21.5 us (0.977)
  Pallas kernels: 21.2 us -> 20.7 us
    pallas_call x1, Pallas kernels: 16.3 us -> 15.8 us  [step_call(): pl.pallas_call(functools.partial(step_kernel, sizes), out_shape=(vmem(gri...]
where the time goes in v4:
time: 21.5 us; the launch traced here: 21.3 us
  Pallas kernels  20.7 us (96%)
  between operations  0.64 us (3%)
    pallas_call x1, Pallas kernels, step_call(): pl.pallas_call(functools.partial(step_kernel, sizes), out_shape=(vmem(gri...  15.8 us
    pallas_call x1, Pallas kernels, force_call(): pl.pallas_call(force_kernel, out_shape=(jax.ShapeDtypeStruct(block, f32),...  4.9 us

profile of v4, /device:TPU:0, one launch (start us, length us, event | category | flops | bytes accessed | tf_op | source)
XLA Modules:
  0.0 21.3 jit_solution(5180286874324457042)
XLA Ops:
  0.6 15.8 %shard_map.67 = (f32[3,34,48,128]{3,2,1,0:T(8,128)S(1)}, f32[3,34,48,128]{3,2,1,0:T(8,128)S(1)}, f32[3,32,2,32,128]{4,3,2,1,0:T(8,128)S(1)}, f32[2,3,32,128]{3,2...) custom-call(s32[3,16]{1,0:T(4,128)} %bitcast.5, ...), custom_call_target="tpu_custom_call" | custom-call | tf_op jit(solution)/shard_map/pallas_call | solution.py:557
  16.4 4.9 %shard_map.68 = (f32[3,32,32,128]{3,2,1,0:T(8,128)}, f32[256,256]{1,0:T(8,128)}, f32[256,256]{1,0:T(8,128)}) custom-call(s32[3,16]{1,0:T(4,128)} %bitcast.6, f32[3,34,48,128]{3,2,1,0:T(8,128)S(1)} %get-tuple-element.14.vel, f32[3,34,48,128]{3,2,1,0:T(8,128)S(1)} %get-tuple-element.15.pred, f32[3,32,2,32,128]{4,3,2,1,0:T(8,128)S(1)} %get-tuple-element.16.near, ...), custom_call_target="tpu_custom_call" | custom-call | tf_op jit(solution)/shard_map/pallas_call | solution.py:690
